TPU v7x, 32 devices: a whole 2x2x4 slice. The times are simulated.
32 devices in a mesh: segment: 2 (over x), blk: 16 (over z, y, core).
Axes of the slice: x: 2, y: 2, z: 4, core: 2. Of those that a mesh axis runs over, the one named last changes fastest.
Arguments:
- pixels: bfloat16 [128, 4, 2048], P('segment', None, 'blk'), may hold values from -6 to 6
- var_group: int32 [128], P('segment'), may hold values from 0 to 7
- var_embed: bfloat16 [128, 2048], P('segment'), may hold values from -3 to 3
- group_weight: bfloat16 [8, 4, 2048], replicated, may hold values from -3 to 3
- agg_query: bfloat16 [2048], replicated, may hold values from -180 to 180
- lat_index: int32 [2048], P('blk'), may hold values from 0 to 359
- lat_table: bfloat16 [360, 2048], replicated, may hold values from -6 to 6
- norm_gain: float32 [2048], replicated, may hold values from 0.1 to 1.9
- w_query: bfloat16 [2048, 1024], P(None, 'segment'), may hold values from -9 to 9
- w_key: bfloat16 [2048, 1024], P(None, 'segment'), may hold values from -0.125 to 0.125
- w_value: bfloat16 [2048, 1024], P(None, 'segment'), may hold values from -0.125 to 0.125
- w_out: bfloat16 [1024, 2048], P('segment'), may hold values from -1.796875 to 1.796875
Outputs:
- aggregated: bfloat16 [2048, 2048], P('blk', 'segment')
- attended: bfloat16 [2048, 2048], P('blk', 'segment')
All inputs are finite; a program needn't handle non-finite values.
Results may differ from a plain program's by a relative error of at most 0.015.
The roundings to bfloat16 on the way count: a program that leaves them out, or rounds other values in their place, can miss the bound.
Values may be sent and summed in bfloat16 or wider, within the bound.
A program may use at most 64 MiB of HBM per device.

v0:
```python
import math

import jax
import jax.numpy as jnp
from jax import lax
from jax.sharding import PartitionSpec as P

HEAD_DIM = 128


def merged(part, axis, combine):
    gathered = jax.tree.map(lambda a: lax.all_gather(a, axis), part)

    def take(source):
        return jax.tree.map(lambda a: lax.dynamic_index_in_dim(a, source, 0, False), gathered)

    return lax.fori_loop(
        1, lax.axis_size(axis), lambda source, state: combine(state, take(source)), take(0)
    )


def combine_parts(first, second):
    peak = jnp.maximum(first[0], second[0])
    scale_first = jnp.exp(first[0] - peak)
    scale_second = jnp.exp(second[0] - peak)
    total = first[1] * scale_first + second[1] * scale_second
    summed = first[2] * scale_first[:, None] + second[2] * scale_second[:, None]
    return (peak, total, summed)


def on_device(
    pixels,
    var_group,
    var_embed,
    group_weight,
    agg_query,
    lat_index,
    lat_table,
    norm_gain,
    w_query,
    w_key,
    w_value,
    w_out,
):
    highest = lax.Precision.HIGHEST
    width = var_embed.shape[1]
    groups = group_weight.shape[0]
    tok_rows = pixels.shape[2]
    lat_rows = lat_table.shape[0]
    sections = lax.axis_size("segment")
    share = width // sections
    start = lax.axis_index("segment") * share
    query32 = agg_query.astype(jnp.float32)
    group32 = group_weight.astype(jnp.float32)
    embed32 = var_embed.astype(jnp.float32)
    pixel32 = pixels.astype(jnp.float32)
    proj_group = jnp.einsum("gpd,d->gp", group32, query32, precision=highest)
    onehot = (var_group[:, None] == jnp.arange(groups, dtype=jnp.int32)[None, :]).astype(
        jnp.float32
    )
    proj_var = jnp.dot(onehot, proj_group, precision=highest)
    offset = jnp.dot(embed32, query32, precision=highest)
    scores = (
        jnp.einsum("vpt,vp->vt", pixel32, proj_var, precision=highest) + offset[:, None]
    ) / math.sqrt(width)
    lat_hot = (lat_index[:, None] == jnp.arange(lat_rows, dtype=jnp.int32)[None, :]).astype(
        jnp.bfloat16
    )
    local_peak = jnp.max(scores, axis=0)
    expo = jnp.exp(scores - local_peak[None, :])
    total = jnp.sum(expo, axis=0)
    grouped = jnp.einsum("vg,vpt->gpt", onehot, expo[:, None, :] * pixel32, precision=highest)
    summed = jnp.einsum("vt,vd->td", expo, embed32, precision=highest)
    summed = summed + jnp.einsum("gpt,gpd->td", grouped, group32, precision=highest)
    local_total = total
    local_sum = summed
    peak, total, summed = merged((local_peak, local_total, local_sum), "segment", combine_parts)
    lat_part = jnp.dot(lat_hot, lat_table, preferred_element_type=jnp.float32)
    latent = summed / total[:, None] + lat_part
    center = latent - jnp.mean(latent, axis=1, keepdims=True)
    spread = jnp.mean(center * center, axis=1, keepdims=True)
    normed = (center * lax.rsqrt(spread + 1e-05) * norm_gain[None, :]).astype(jnp.bfloat16)
    latent_share = lax.dynamic_slice_in_dim(latent, start, share, 1)
    aggregated = latent_share.astype(jnp.bfloat16)
    queries = jnp.dot(normed, w_query, preferred_element_type=jnp.float32).astype(jnp.bfloat16)
    keys = jnp.dot(normed, w_key, preferred_element_type=jnp.float32).astype(jnp.bfloat16)
    values = jnp.dot(normed, w_value, preferred_element_type=jnp.float32).astype(jnp.bfloat16)
    head_count = queries.shape[1] // HEAD_DIM
    query_heads = queries.reshape(tok_rows, head_count, HEAD_DIM)
    scale = 1.0 / math.sqrt(HEAD_DIM)

    def attend(carry, key_heads, value_heads):
        running, total, accum = carry
        logits = (
            jnp.einsum("thd,rhd->thr", query_heads, key_heads, preferred_element_type=jnp.float32)
            * scale
        )
        fresh = jnp.maximum(running, jnp.max(logits, axis=2))
        shrink = jnp.exp(running - fresh)
        expo = jnp.exp(logits - fresh[:, :, None])
        total = total * shrink + jnp.sum(expo, axis=2)
        mixed = jnp.einsum(
            "thr,rhd->thd",
            expo.astype(jnp.bfloat16),
            value_heads,
            preferred_element_type=jnp.float32,
        )
        accum = accum * shrink[:, :, None] + mixed
        return (fresh, total, accum)

    start_state = (
        jnp.full((tok_rows, head_count), -1e30, jnp.float32),
        jnp.zeros((tok_rows, head_count), jnp.float32),
        jnp.zeros((tok_rows, head_count, HEAD_DIM), jnp.float32),
    )
    carry = start_state
    key_rows = lax.all_gather(keys, "blk", axis=0, tiled=True)
    value_rows = lax.all_gather(values, "blk", axis=0, tiled=True)
    rows = key_rows.shape[0]
    block = 2048
    key_blocks = key_rows.reshape(rows // block, block, head_count, HEAD_DIM)
    value_blocks = value_rows.reshape(rows // block, block, head_count, HEAD_DIM)

    def one_block(state, blocks):
        return (attend(state, blocks[0], blocks[1]), None)

    carry, unused = lax.scan(one_block, carry, (key_blocks, value_blocks))
    running, total, accum = carry
    heads_out = (
        (accum / total[:, :, None]).reshape(tok_rows, head_count * HEAD_DIM).astype(jnp.bfloat16)
    )
    partial_value = jnp.dot(heads_out, w_out, preferred_element_type=jnp.float32)
    attended = lax.psum_scatter(
        partial_value.astype(jnp.bfloat16), "segment", scatter_dimension=1, tiled=True
    )
    return (aggregated, attended)


def solution(mesh):
    in_specs = (
        P("segment", None, "blk"),
        P("segment"),
        P("segment", None),
        P(),
        P(),
        P("blk"),
        P(),
        P(),
        P(None, "segment"),
        P(None, "segment"),
        P(None, "segment"),
        P("segment", None),
    )
    out_specs = (P("blk", "segment"), P("blk", "segment"))
    return jax.shard_map(
        on_device, mesh=mesh, in_specs=in_specs, out_specs=out_specs, check_vma=False
    )
```

profile of v0, /device:TPU:0, one launch (start us, length us, event | category | flops | bytes accessed | tf_op | source)
XLA Modules:
  0.0 174.4 jit_solution(17387931946372268658)
XLA Ops:
  7.2 0.9 reshape.118
  8.1 0.7 reshape.114
  8.8 1.1 convolution_bitcast_fusion.1
  9.9 1.6 fusion.48
  11.5 0.9 fusion.32
  12.4 1.2 fusion.49
  13.7 0.1 fusion.46
  13.8 0.9 convert_multiply_fusion
  14.7 0.9 fusion.27
  15.6 1.5 convolution_bitcast_fusion
  17.1 1.6 convolution_add_fusion.1
  18.8 5.2 %all-gather.4 = f32[2,1,128]{2,1,0:T(1,128)S(1)} all-gather(f32[1,1,128]{2,1,0:T(1,128)S(1)} %bitcast.113), channel_id=4, replica_groups=mesh['segment'=2,'blk'=16] {'segment'}, dimensions={0}, use_global_device_ids=true | all-gather | bytes 1536 | tf_op jit(solution)/shard_map/all_gather | solution.py:12
  24.0 4.2 %all-gather.3 = f32[2,1,128]{2,1,0:T(1,128)S(1)} all-gather(f32[1,1,128]{2,1,0:T(1,128)S(1)} %bitcast.112), channel_id=3, replica_groups=mesh['segment'=2,'blk'=16] {'segment'}, dimensions={0}, use_global_device_ids=true | all-gather | bytes 1536 | tf_op jit(solution)/shard_map/all_gather | solution.py:12
  28.2 26.5 %all-gather.13.cloned.1.call-done = f32[256,2048]{1,0:T(8,128)} async-done(((f32[128,2048]{1,0:T(8,128)}), f32[256,2048]{1,0:T(8,128)}) %all-gather.13.cloned.1.call-update) | async-done | bytes 2097168 | tf_op jit(solution)/shard_map/all_gather | solution.py:12
  54.8 2.6 %fusion.47 = (f32[128]{0:T(128)S(1)}, f32[128,2048]{1,0:T(8,128)S(1)}) fusion(bf16[360,2048]{1,0:T(8,128)(2,1)} %param.18, s32[128]{0:T(128)S(1)} %copy-done.6, f32[128]{0:T(128)S(1)} %get-tuple-element.33, f32[128]{0:T(128)S(1)} %get-tuple-element.35, f32[256,2048]{1,0:T(8,128)} %all-gather.13.cloned.1.call-done, f32[128]{0:T(128)S(1)} %get-tuple-element.34), kind=kOutput, calls=%fused_computation.65 | convolution fusion | flops 190362496 | bytes 4622848 | tf_op jit(solution)/shard_map/dot_general | solution.py:78
  57.4 0.3 multiply_reduce_fusion
  57.6 0.8 copy-done.2
  58.4 0.2 multiply_convert_fusion
  58.6 0.7 copy-done.3
  59.3 1.1 convolution_convert_fusion.3
  60.5 2.7 %convolution_convert_fusion.1 = bf16[128,512]{1,0:T(8,128)(2,1)} fusion(bf16[128,2048]{1,0:T(8,128)(2,1)S(1)} %multiply_convert_fusion, bf16[2048,512]{1,0:T(8,128)(2,1)} %param.22), kind=kOutput, calls=%fused_computation.17 | convolution fusion | flops 268500992 | bytes 2752512 | tf_op jit(solution)/shard_map/dot_general | solution.py:87
  63.3 2.0 %fusion.16 = bf16[16,4,8,128]{3,2,1,0:T(8,128)(2,1)S(1)} fusion(bf16[128,2048]{1,0:T(8,128)(2,1)S(1)} %multiply_convert_fusion, bf16[2048,512]{1,0:T(8,128)(2,1)} %param.20), kind=kOutput, calls=%fused_computation.20 | convolution fusion | flops 268500992 | bytes 2752512 | tf_op jit(solution)/shard_map/dot_general | solution.py:85
  65.3 36.8 %all-gather.9.cloned.1.call-done = bf16[2048,512]{1,0:T(8,128)(2,1)} async-done(((bf16[128,512]{1,0:T(8,128)(2,1)}), bf16[2048,512]{1,0:T(8,128)(2,1)}) %all-gather.9.cloned.1.call-update) | async-done | bytes 2097168 | tf_op jit(solution)/shard_map/all_gather | solution.py:117
  102.1 2.3 %bitcast_reduce_fusion = (f32[128,4]{0,1:T(4,128)S(1)}, f32[4,2048,128]{2,1,0:T(8,128)S(1)}) fusion(bf16[16,4,8,128]{3,2,1,0:T(8,128)(2,1)S(1)} %fusion.16, bf16[2048,512]{1,0:T(8,128)(2,1)} %all-gather.9.cloned.1.call-done), kind=kOutput, calls=%fused_computation.1 | convolution fusion | flops 270532096 | bytes 6424576 | tf_op jit(solution)/shard_map/while/body/eval_jaxpr/thd,rhd->thr/dot_general | solution.py:95
  104.5 0.7 fusion.1
  105.2 1.2 copy-done.1
  106.4 38.7 %all-gather.11.cloned.1.call-done = bf16[2048,512]{1,0:T(8,128)(2,1)} async-done(((bf16[128,512]{1,0:T(8,128)(2,1)}), bf16[2048,512]{1,0:T(8,128)(2,1)}) %all-gather.11.cloned.1.call-update) | async-done | bytes 2097168 | tf_op jit(solution)/shard_map/all_gather | solution.py:118
  145.1 4.0 %copy.29 = bf16[2048,512]{0,1:T(8,128)(2,1)} copy(bf16[2048,512]{1,0:T(8,128)(2,1)} %all-gather.11.cloned.1.call-done) | data formatting | bytes 4194304 | tf_op jit(solution)/shard_map/while/body/jit(dynamic_index_in_dim)/squeeze | solution.py:127
  149.1 4.0 %fusion.20 = bf16[128,4,128]{0,2,1:T(8,128)(2,1)S(1)} fusion(bf16[2048,4,128]{0,2,1:T(8,128)(2,1)} %bitcast.108, f32[4,2048,128]{2,1,0:T(8,128)} %copy-done.1, f32[128,4]{0,1:T(4,128)S(1)} %broadcast_maximum_fusion, f32[128,4]{0,1:T(4,128)S(1)} %get-tuple-element.46, f32[128,4]{0,1:T(4,128)S(1)} %get-tuple-element.38), kind=kOutput, calls=%fused_computation.23 | convolution fusion | flops 271777792 | bytes 6428672 | tf_op jit(solution)/shard_map/while/body/eval_jaxpr/thr,rhd->thd/dot_general | solution.py:102
  153.1 1.3 convolution_convert_fusion
  154.4 1.8 %dynamic-slice_convert_fusion = bf16[128,1024]{1,0:T(8,128)(2,1)} fusion(f32[128,2048]{1,0:T(8,128)} %copy-done.2, s32[]{:T(128)S(6)} %select_n.12), kind=kLoop, calls=%fused_computation.30 | loop fusion | bytes 524292 | tf_op jit(solution)/shard_map/convert_element_type | solution.py:84
  156.2 11.7 %reduce-scatter.2.cloned.1.call-done = bf16[128,1024]{1,0:T(8,128)(2,1)} async-done(((bf16[128,2048]{1,0:T(8,128)(2,1)}), bf16[128,1024]{1,0:T(8,128)(2,1)}) %reduce-scatter.2.cloned.1.call-update) | async-done | bytes 262160 | tf_op jit(solution)/shard_map/reduce_scatter | solution.py:133
  (25 shorter events, 0.4 us)
Async XLA Ops:
  7.2 145.9 %copy-start = (bf16[512,2048]{1,0:T(8,128)(2,1)S(1)}, bf16[512,2048]{1,0:T(8,128)(2,1)}, u32[]{:S(2)}) copy-start(bf16[512,2048]{1,0:T(8,128)(2,1)} %param.23) | copy-start | bytes 6291460
  7.2 10.0 %copy-start.4 = (bf16[64,2048]{1,0:T(8,128)(2,1)S(1)}, bf16[64,2048]{1,0:T(8,128)(2,1)}, u32[]{:S(2)}) copy-start(bf16[64,2048]{1,0:T(8,128)(2,1)} %param.14) | copy-start | bytes 786436
  7.2 47.6 %all-gather.13.cloned.1.call-start = ((), (), s32[]{:S(2)}) async-start(), calls=%async_computation.4 | async-start | bytes 3145728 | tf_op jit(solution)/shard_map/all_gather | solution.py:12
  15.6 39.2 %copy-start.6 = (s32[128]{0:T(128)S(1)}, s32[128]{0:T(128)}, u32[]{:S(2)}) copy-start(s32[128]{0:T(128)} %param.17) | copy-start | bytes 1540
  18.8 83.3 %all-gather.9.cloned.1.call-start = ((), (), s32[]{:S(2)}) async-start(), calls=%async_computation.1 | async-start | bytes 2228224 | tf_op jit(solution)/shard_map/all_gather | solution.py:117
  54.8 3.6 %copy-start.5 = (f32[2048]{0:T(1024)S(1)}, f32[2048]{0:T(1024)}, u32[]{:S(2)}) copy-start(f32[2048]{0:T(1024)} %param.19) | copy-start | bytes 24580
  57.4 1.1 copy-start.2
  57.4 2.0 %copy-start.3 = (bf16[2048,512]{1,0:T(8,128)(2,1)S(1)}, bf16[2048,512]{1,0:T(8,128)(2,1)}, u32[]{:S(2)}) copy-start(bf16[2048,512]{1,0:T(8,128)(2,1)} %param.21) | copy-start | bytes 6291460
  60.5 84.6 %all-gather.11.cloned.1.call-start = ((), (), s32[]{:S(2)}) async-start(), calls=%async_computation.2 | async-start | bytes 2228224 | tf_op jit(solution)/shard_map/all_gather | solution.py:118
  63.2 104.6 %reduce-scatter.2.cloned.1.call-start = ((), (), s32[]{:S(2)}) async-start(), calls=%async_computation.3 | async-start | bytes 786432 | tf_op jit(solution)/shard_map/reduce_scatter | solution.py:133
  104.5 1.9 %copy-start.1 = (f32[4,2048,128]{2,1,0:T(8,128)}, f32[4,2048,128]{2,1,0:T(8,128)S(1)}, u32[]{:S(2)}) copy-start(f32[4,2048,128]{2,1,0:T(8,128)S(1)} %get-tuple-element.50) | copy-start | bytes 12582916
Sparse Core Ops, SparseCore 0:
  18.9 35.8 all-gather.12
  60.6 41.4 all-gather.8
  104.9 40.1 all-gather.10
  154.5 13.3 reduce-scatter.1
where the time goes:
time: 175 us; the launch traced here: 174 us
  waiting for transfers between devices  114 us (65%)
  matrix products  24.9 us (14%)
  between operations  13.9 us (8%)
  local copies, waits for them, and re-layouts  10.1 us (6%)
  blocking collectives  9.39 us (5%)
  other arithmetic  2.26 us (1%)
    all_gather x1, waiting for transfers between devices, on_device(): value_rows = lax.all_gather(values, 'blk', axis=0, tiled=True)  38.7 us
    all_gather x1, waiting for transfers between devices, on_device(): key_rows = lax.all_gather(keys, 'blk', axis=0, tiled=True)  36.8 us
    all_gather x1, waiting for transfers between devices, merged(): gathered = jax.tree.map(lambda a: lax.all_gather(a, axis), part)  26.5 us
    reduce_scatter x1, waiting for transfers between devices, on_device(): lax.psum_scatter(partial_value.astype(jnp.bfloat16), 'segment', scatter_d...  11.7 us
    all_gather x2, blocking collectives, merged(): gathered = jax.tree.map(lambda a: lax.all_gather(a, axis), part)  9.39 us
    unnamed x16, local copies, waits for them, and re-layouts  4.29 us
    squeeze x1, local copies, waits for them, and re-layouts, on_device(): carry, unused = lax.scan(one_block, carry, (key_blocks, value_blocks))  3.99 us
    dot_general x1, matrix products, attend(): jnp.einsum('thr,rhd->thd', expo.astype(jnp.bfloat16), value_heads, prefer...  3.99 us
  transfers between devices with their start and end apart: 4, of which 4 were waited for; matrix products, arithmetic and copies ran while one was open for 5% of the time, Pallas kernels for 0%

commit v1 on v0

v1 whole, which is shorter than its diff:
```python
import functools
import math

import jax
import jax.numpy as jnp
from jax import lax
from jax.experimental import pallas as pl
from jax.experimental.pallas import tpu as pltpu
from jax.sharding import PartitionSpec as P

HEAD_DIM = 128
MESH = pl.DeviceIdType.MESH
F32 = jnp.float32
BF16 = jnp.bfloat16


def kernel(
    S, R, C,
    pix_ref, vg_ref, emb_ref, gw_ref, q_ref, lidx_ref, lat_ref, gain_ref,
    wq_ref, wk_ref, wv_ref, wo_ref,
    agg_ref, att_ref,
    bm, latv, wqv, wkv, wvv, woa, gtmp, pixf, cf, ck, lt, nm, kv, qs, ms, ls, acc, ho,
    loc, e_s, e_r, ep_s, ep_r, c_s, c_r, o_s, o_r, op_s, op_r, h_s, h_r, k_s, k_r,
):
    D = emb_ref.shape[1]
    Vl = emb_ref.shape[0]
    G, PX, _ = gw_ref.shape
    GP = G * PX
    T = pix_ref.shape[2]
    NL = lat_ref.shape[0]
    Cl = wq_ref.shape[1]
    H = Cl // HEAD_DIM
    share = D // S
    half = D // 2
    clh = Cl // 2
    Kp = ck.shape[0]
    W = C * 2 * T
    s = lax.axis_index("segment")
    b = lax.axis_index("blk")
    c = lax.rem(b, 2)
    rc = b // 2
    col = lax.rem(rc, C)
    r = rc // C
    partner = b + 1 - 2 * c

    def dev(seg, blk):
        return {"segment": seg, "blk": blk}

    barrier = pltpu.get_barrier_semaphore()

    def greet(seg, blk):
        pl.semaphore_signal(barrier, inc=1, device_id=dev(seg, blk), device_id_type=MESH)

    for k in range(1, S):
        greet(lax.rem(s + k, S), b)
    greet(s, partner)
    pl.when(r > 0)(lambda: greet(s, b - 2 * C))
    pl.when(r < R - 1)(lambda: greet(s, b + 2 * C))
    pl.when(col > 0)(lambda: greet(s, b - 2))
    pl.when(col < C - 1)(lambda: greet(s, b + 2))

    own_rows = pl.ds(pl.multiple_of(s * Vl, Vl), Vl)
    locals_ = [
        pltpu.make_async_copy(emb_ref, bm.at[own_rows], loc.at[0]),
        pltpu.make_async_copy(lat_ref, latv, loc.at[1]),
        pltpu.make_async_copy(wk_ref, wkv, loc.at[2]),
        pltpu.make_async_copy(wv_ref, wvv, loc.at[3]),
        pltpu.make_async_copy(wq_ref, wqv, loc.at[4]),
        pltpu.make_async_copy(
            wo_ref.at[:, pl.ds(pl.multiple_of(s * share, share), share)], woa.at[s], loc.at[5]
        ),
    ]
    for one in locals_:
        one.start()
    count = (
        S
        + jnp.minimum(r, 1)
        + jnp.minimum(R - 1 - r, 1)
        + jnp.minimum(col, 1)
        + jnp.minimum(C - 1 - col, 1)
    )
    pl.semaphore_wait(barrier, count)

    def remote(src, dst, send, recv, seg, blk):
        return pltpu.make_async_remote_copy(
            src_ref=src, dst_ref=dst, send_sem=send, recv_sem=recv,
            device_id=dev(seg, blk), device_id_type=MESH,
        )

    def seg_at(k):
        return lax.rem(s + k, S)

    def emb_region(seg, core):
        return bm.at[
            pl.ds(pl.multiple_of(seg * Vl, Vl), Vl), pl.ds(pl.multiple_of(core * half, half), half)
        ]

    my_half = pl.ds(pl.multiple_of(c * half, half), half)
    e_out = [
        remote(emb_ref.at[:, my_half], emb_region(s, c), e_s.at[k], e_r.at[k], seg_at(k), b)
        for k in range(1, S)
    ]
    for one in e_out:
        one.start()

    q = q_ref[...]
    for g in range(G):
        one_group = gw_ref[g].astype(F32)
        for p in range(PX):
            gtmp[p * G + g : p * G + g + 1, :] = one_group[p : p + 1, :]
    gwp = gtmp[...]
    bm[S * Vl : S * Vl + GP, :] = gwp.astype(BF16)
    if Kp > S * Vl + GP:
        bm[S * Vl + GP : Kp, :] = jnp.zeros((Kp - S * Vl - GP, D), BF16)
    pg = jnp.sum(gwp * q, axis=1, keepdims=True)
    for v in range(Vl):
        pixf[PX * v : PX * v + PX, :] = pix_ref[v].astype(F32)
    vg = vg_ref[...]
    row_at = lax.broadcasted_iota(jnp.int32, (Vl, Vl), 0)
    col_at = lax.broadcasted_iota(jnp.int32, (Vl, Vl), 1)
    vcol = jnp.sum(jnp.where(row_at == col_at, vg.astype(F32), 0.0), axis=1, keepdims=True)
    onehot = (lax.broadcasted_iota(jnp.int32, (G, Vl), 0) == vg).astype(F32)
    locals_[0].wait()
    scores = jnp.sum(bm[own_rows, :].astype(F32) * q, axis=1, keepdims=True)
    planes = [pixf[pl.ds(p, Vl, stride=PX), :] for p in range(PX)]
    for p in range(PX):
        pv = jnp.zeros((Vl, 1), F32)
        for g in range(G):
            pv = jnp.where(vcol == float(g), pg[p * G + g : p * G + g + 1, :], pv)
        scores = scores + planes[p] * pv
    scores = scores / math.sqrt(D)
    peak = jnp.max(scores, axis=0, keepdims=True)
    expo = jnp.exp(scores - peak)
    cf[s, 0:Vl, :] = expo
    for p in range(PX):
        cf[s, Vl + p * G : Vl + p * G + G, :] = jnp.dot(
            onehot, expo * planes[p], precision=lax.Precision.HIGHEST, preferred_element_type=F32
        )
    top = Vl + GP
    cf[s, top : top + 8, :] = jnp.broadcast_to(peak, (8, T))
    cf[s, top + 8 : top + 16, :] = jnp.broadcast_to(jnp.sum(expo, axis=0, keepdims=True), (8, T))
    c_out = [
        remote(cf.at[s], cf.at[s], c_s.at[k], c_r.at[k], seg_at(k), b) for k in range(1, S)
    ]
    for one in c_out:
        one.start()

    def wo_rows(core):
        return pl.ds(pl.multiple_of(core * clh, clh), clh)

    o_out = [
        remote(
            wo_ref.at[wo_rows(c), pl.ds(pl.multiple_of(seg_at(k) * share, share), share)],
            woa.at[s, wo_rows(c)], o_s.at[k], o_r.at[k], seg_at(k), b,
        )
        for k in range(1, S)
    ]
    for one in o_out:
        one.start()

    lat_rows = ((NL + 127) // 128) * 128
    hot = (lax.broadcasted_iota(jnp.int32, (lat_rows, T), 0) == lidx_ref[...]).astype(F32)
    hot = hot.T.astype(BF16)[:, :NL]

    ep_out = []
    for k in range(1, S):
        src = seg_at(S - k)
        remote(emb_region(src, c), emb_region(src, c), e_s.at[k], e_r.at[k], s, partner).wait_recv()
        one = remote(
            emb_region(src, c), emb_region(src, c), ep_s.at[k], ep_r.at[k], s, partner
        )
        one.start()
        ep_out.append(one)
    for k in range(1, S):
        src = seg_at(S - k)
        remote(cf.at[src], cf.at[src], c_s.at[k], c_r.at[k], s, partner).wait_recv()
    best = cf[0, top : top + 1, :]
    for k in range(1, S):
        best = jnp.maximum(best, cf[k, top : top + 1, :])
    factors = [jnp.exp(cf[k, top : top + 1, :] - best) for k in range(S)]
    total = factors[0] * cf[0, top + 8 : top + 9, :]
    for k in range(1, S):
        total = total + factors[k] * cf[k, top + 8 : top + 9, :]
    grouped = jnp.zeros((GP, T), F32)
    for k in range(S):
        share_k = factors[k] / total
        ck[k * Vl : k * Vl + Vl, :] = cf[k, 0:Vl, :] * share_k
        grouped = grouped + cf[k, Vl : Vl + GP, :] * share_k
    ck[S * Vl : S * Vl + GP, :] = grouped
    if Kp > S * Vl + GP:
        ck[S * Vl + GP : Kp, :] = jnp.zeros((Kp - S * Vl - GP, T), F32)
    ct = ck[...].T
    hi = ct.astype(BF16)
    rest = ct - hi.astype(F32)
    mid = rest.astype(BF16)
    low = (rest - mid.astype(F32)).astype(BF16)
    for k in range(1, S):
        src = seg_at(S - k)
        other = emb_region(src, 1 - c)
        remote(other, other, ep_s.at[k], ep_r.at[k], s, partner).wait_recv()
    locals_[1].wait()
    step = 512
    mean = jnp.zeros((T, 1), F32)
    for j in range(D // step):
        at = slice(j * step, (j + 1) * step)
        base = bm[:, at]
        part = jnp.dot(low, base, preferred_element_type=F32)
        part = part + jnp.dot(mid, base, preferred_element_type=F32)
        part = part + jnp.dot(hi, base, preferred_element_type=F32)
        part = part + jnp.dot(hot, latv[:, at], preferred_element_type=F32)
        lt[:, at] = part
        mean = mean + jnp.sum(part, axis=1, keepdims=True)
    mean = mean / D
    spread = jnp.zeros((T, 1), F32)
    for j in range(D // step):
        center = lt[:, j * step : (j + 1) * step] - mean
        spread = spread + jnp.sum(center * center, axis=1, keepdims=True)
    inv = lax.rsqrt(spread / D + 1e-05)
    for j in range(D // step):
        at = slice(j * step, (j + 1) * step)
        nm[:, at] = ((lt[:, at] - mean) * inv * gain_ref[:, at]).astype(BF16)

    def region(part, blk):
        return kv.at[part, pl.ds(pl.multiple_of(blk * T, T), T)]

    def sends(r0, c0, act):
        blk = (r0 * C + c0) * 2 + c
        here = c0 == col

        def each(part, way, to):
            return remote(
                region(part, blk), region(part, blk), k_s.at[way, part, blk], k_r.at[part, blk],
                s, to,
            )

        def go(part):
            pl.when(here & (r > 0) & (r0 >= r))(lambda: act(each(part, 0, b - 2 * C)))
            pl.when(here & (r < R - 1) & (r0 <= r))(lambda: act(each(part, 1, b + 2 * C)))
            pl.when((col > 0) & (c0 >= col))(lambda: act(each(part, 2, b - 2)))
            pl.when((col < C - 1) & (c0 <= col))(lambda: act(each(part, 3, b + 2)))
            act(each(part, 4, partner))

        return go

    def start(copy):
        copy.start()

    def arrived(part, blk):
        remote(
            region(part, blk), region(part, blk), k_s.at[4, part, blk], k_r.at[part, blk],
            s, partner,
        ).wait_recv()

    mine = sends(r, col, start)
    own_keys = pl.ds(pl.multiple_of(b * T, T), T)
    locals_[2].wait()
    kv[0, own_keys, :] = jnp.dot(nm[...], wkv[...], preferred_element_type=F32).astype(BF16)
    mine(0)
    locals_[3].wait()
    kv[1, own_keys, :] = jnp.dot(nm[...], wvv[...], preferred_element_type=F32).astype(BF16)
    mine(1)
    locals_[4].wait()
    qs[...] = jnp.dot(nm[...], wqv[...], preferred_element_type=F32).astype(BF16)
    agg_ref[...] = lt[:, pl.ds(pl.multiple_of(s * share, share), share)].astype(BF16)
    ms[...] = jnp.full(ms.shape, -1e30, F32)
    ls[...] = jnp.zeros(ls.shape, F32)
    acc[...] = jnp.zeros(acc.shape, F32)
    scale = 1.0 / math.sqrt(HEAD_DIM)

    def attend(row):
        keys_at = pl.ds(pl.multiple_of(row * W, W), W)
        for h in range(H):
            cols = slice(h * HEAD_DIM, (h + 1) * HEAD_DIM)
            logits = (
                lax.dot_general(
                    qs[:, cols], kv[0, keys_at, cols], (((1,), (1,)), ((), ())),
                    preferred_element_type=F32,
                )
                * scale
            )
            old = ms[h]
            fresh = jnp.maximum(old, jnp.max(logits, axis=1, keepdims=True))
            shrink = jnp.exp(old - fresh)
            expo = jnp.exp(logits - fresh[:, 0:1])
            ls[h] = ls[h] * shrink + jnp.sum(expo, axis=1, keepdims=True)
            ms[h] = fresh
            acc[:, cols] = acc[:, cols] * shrink[:, 0:1] + jnp.dot(
                expo.astype(BF16), kv[1, keys_at, cols], preferred_element_type=F32
            )

    def from_column(row):
        for part in range(2):
            arrived(part, (row * C + col) * 2 + c)
            sends(row, col, start)(part)

    def finish(row):
        for dist in range(1, C):
            for way in (-1, 1):
                c0 = col + way * dist

                @pl.when((c0 >= 0) & (c0 < C))
                def _():
                    for part in range(2):
                        arrived(part, (row * C + c0) * 2 + c)
                        sends(row, c0, start)(part)

        for c0 in range(C):
            for part in range(2):
                arrived(part, (row * C + c0) * 2 + 1 - c)
        attend(row)

    def stage(d, carry):
        def ahead(way, inner):
            row = r + (2 * way - 1) * (d + 1)
            pl.when((row >= 0) & (row < R))(lambda: from_column(row))
            return inner

        lax.fori_loop(0, 2, ahead, 0)

        def now(way, inner):
            row = r + (2 * way - 1) * d
            pl.when((row >= 0) & (row < R) & (d + way > 0))(lambda: finish(row))
            return inner

        lax.fori_loop(0, 2, now, 0)
        return carry

    lax.fori_loop(0, R, stage, 0)

    for h in range(H):
        cols = slice(h * HEAD_DIM, (h + 1) * HEAD_DIM)
        ho[s, :, cols] = (acc[:, cols] / ls[h][:, 0:1]).astype(BF16)
    h_out = [remote(ho.at[s], ho.at[s], h_s.at[k], h_r.at[k], seg_at(k), b) for k in range(1, S)]
    for one in h_out:
        one.start()
    op_out = []
    for k in range(1, S):
        src = seg_at(S - k)
        block = woa.at[src, wo_rows(c)]
        remote(block, block, o_s.at[k], o_r.at[k], s, partner).wait_recv()
        one = remote(block, block, op_s.at[k], op_r.at[k], s, partner)
        one.start()
        op_out.append(one)
    locals_[5].wait()
    lt[:, 0:share] = jnp.dot(ho[s], woa[s], preferred_element_type=F32)
    for k in range(1, S):
        src = seg_at(S - k)
        block = woa.at[src, wo_rows(1 - c)]
        remote(block, block, op_s.at[k], op_r.at[k], s, partner).wait_recv()
        remote(ho.at[src], ho.at[src], h_s.at[k], h_r.at[k], s, partner).wait_recv()
        lt[:, 0:share] = lt[:, 0:share] + jnp.dot(ho[src], woa[src], preferred_element_type=F32)
    att_ref[...] = lt[:, 0:share].astype(BF16)

    for one in e_out + ep_out + c_out + o_out + op_out + h_out:
        one.wait_send()

    def drain(i, carry):
        ends = sends(i // C, lax.rem(i, C), lambda copy: copy.wait_send())
        ends(0)
        ends(1)
        return carry

    lax.fori_loop(0, R * C, drain, 0)


def solution(mesh):
    S = mesh.shape["segment"]
    B = mesh.shape["blk"]
    chips = B // 2
    C = 1
    while C * C * 4 <= chips:
        C *= 2
    R = chips // C

    def on_device(
        pixels, var_group, var_embed, group_weight, agg_query, lat_index, lat_table, norm_gain,
        w_query, w_key, w_value, w_out,
    ):
        vl, D = var_embed.shape
        G, PX, _ = group_weight.shape
        T = pixels.shape[2]
        NL = lat_table.shape[0]
        cl = w_query.shape[1]
        H = cl // HEAD_DIM
        share = D // S
        kp = ((S * vl + G * PX + 127) // 128) * 128
        vm = pl.BlockSpec(memory_space=pltpu.VMEM)
        far = pl.BlockSpec(memory_space=pl.ANY)
        dma = pltpu.SemaphoreType.DMA
        out = jax.ShapeDtypeStruct((T, share), BF16)
        return pl.pallas_call(
            functools.partial(kernel, S, R, C),
            out_shape=(out, out),
            in_specs=[vm, vm, far, vm, vm, vm, far, vm, far, far, far, far],
            out_specs=(vm, vm),
            scratch_shapes=[
                pltpu.VMEM((kp, D), BF16),
                pltpu.VMEM((NL, D), BF16),
                pltpu.VMEM((D, cl), BF16),
                pltpu.VMEM((D, cl), BF16),
                pltpu.VMEM((D, cl), BF16),
                pltpu.VMEM((S, cl, share), BF16),
                pltpu.VMEM((G * PX, D), F32),
                pltpu.VMEM((vl * PX, T), F32),
                pltpu.VMEM((S, vl + G * PX + 16, T), F32),
                pltpu.VMEM((kp, T), F32),
                pltpu.VMEM((T, D), F32),
                pltpu.VMEM((T, D), BF16),
                pltpu.VMEM((2, B * T, cl), BF16),
                pltpu.VMEM((T, cl), BF16),
                pltpu.VMEM((H, T, 128), F32),
                pltpu.VMEM((H, T, 128), F32),
                pltpu.VMEM((T, cl), F32),
                pltpu.VMEM((S, T, cl), BF16),
                dma((6,)),
            ]
            + [dma((S,))] * 12
            + [dma((5, 2, B)), dma((2, B))],
            compiler_params=pltpu.CompilerParams(
                collective_id=0, has_side_effects=True, vmem_limit_bytes=48 * 1024 * 1024
            ),
        )(
            pixels,
            var_group.reshape(1, vl),
            var_embed,
            group_weight,
            agg_query.astype(F32).reshape(1, D),
            lat_index.reshape(1, T),
            lat_table,
            norm_gain.reshape(1, D),
            w_query,
            w_key,
            w_value,
            w_out,
        )

    in_specs = (
        P("segment", None, "blk"), P("segment"), P("segment", None), P(), P(), P("blk"), P(), P(),
        P(None, "segment"), P(None, "segment"), P(None, "segment"), P("segment", None),
    )
    out_specs = (P("blk", "segment"), P("blk", "segment"))
    return jax.shard_map(
        on_device, mesh=mesh, in_specs=in_specs, out_specs=out_specs, check_vma=False
    )
```

time: 175 us -> 57.3 us (0.33)
  waiting for transfers between devices: 114 us -> 0 us
  Pallas kernels: 0 us -> 46.6 us
  matrix products: 24.9 us -> 0 us
  between operations: 13.9 us -> 0.65 us
  blocking collectives: 9.39 us -> 0 us
    all_gather x3 -> x0, waiting for transfers between devices: 102 us -> none  [the longest x1 38.7 us: on_device(): value_rows = lax.all_gather(values, 'blk', axis=0, tiled=True)]
    pallas_call x0 -> x1, Pallas kernels: none -> 46.6 us  [on_device(): pl.pallas_call(functools.partial(kernel, S, R, C), out_shape=(out, out),...]
    dot_general x14 -> x0, matrix products: 24.9 us -> none  [the longest x1 3.99 us: attend(): jnp.einsum('thr,rhd->thd', expo.astype(jnp.bfloat16), value_heads, prefer...]
    reduce_scatter x1 -> x0, waiting for transfers between devices: 11.7 us -> none  [on_device(): lax.psum_scatter(partial_value.astype(jnp.bfloat16), 'segment', scatter_d...]
    all_gather x2 -> x0, blocking collectives: 9.39 us -> none  [merged(): gathered = jax.tree.map(lambda a: lax.all_gather(a, axis), part)]
    unnamed x16 -> x18, local copies, waits for them, and re-layouts: 4.29 us -> 9.07 us
    squeeze x1 -> x0, local copies, waits for them, and re-layouts: 3.99 us -> none  [on_device(): carry, unused = lax.scan(one_block, carry, (key_blocks, value_blocks))]
    convert_element_type x1 -> x0, local copies, waits for them, and re-layouts: 1.78 us -> none  [on_device(): aggregated = latent_share.astype(jnp.bfloat16)]
  transfers between devices with their start and end apart: 4 -> 0, of which waited for: 4 -> 0; matrix products, arithmetic and copies ran while one was open for 5% -> 0% of each run, Pallas kernels for 0% -> 0%
where the time goes in v1:
time: 57.3 us; the launch traced here: 57 us
  Pallas kernels  46.6 us (81%)
  local copies, waits for them, and re-layouts  9.07 us (16%)
  other arithmetic  0.69 us (1%)
  between operations  0.65 us (1%)
    pallas_call x1, Pallas kernels, on_device(): pl.pallas_call(functools.partial(kernel, S, R, C), out_shape=(out, out),...  46.6 us
    unnamed x18, local copies, waits for them, and re-layouts  9.07 us

profile of v1, /device:TPU:0, one launch (start us, length us, event | category | flops | bytes accessed | tf_op | source)
XLA Modules:
  0.0 57.0 jit_solution(8850841564796101951)
XLA Ops:
  0.6 0.7 %reshape.23 = f32[2048]{0:T(1024)S(1)} convert(bf16[2048]{0:T(1024)(128)(2,1)} %param.16) | non-fusion elementwise | flops 2048 | bytes 12288 | tf_op jit(solution)/shard_map/reshape | solution.py:427
  1.3 0.0 copy-start
  1.3 1.6 %copy-done = bf16[2048,512]{1,0:T(8,128)(2,1)S(1)} copy-done((bf16[2048,512]{1,0:T(8,128)(2,1)S(1)}, bf16[2048,512]{1,0:T(8,128)(2,1)}, u32[]{:S(2)}) %copy-start) | copy-done | bytes 2097176
  2.9 0.0 copy-start.1
  2.9 1.4 %copy-done.1 = bf16[360,2048]{1,0:T(8,128)(2,1)S(1)} copy-done((bf16[360,2048]{1,0:T(8,128)(2,1)S(1)}, bf16[360,2048]{1,0:T(8,128)(2,1)}, u32[]{:S(2)}) %copy-start.1) | copy-done | bytes 1474584
  4.3 0.0 copy-start.2
  4.3 0.9 %copy-done.2 = bf16[64,2048]{1,0:T(8,128)(2,1)S(1)} copy-done((bf16[64,2048]{1,0:T(8,128)(2,1)S(1)}, bf16[64,2048]{1,0:T(8,128)(2,1)}, u32[]{:S(2)}) %copy-start.2) | copy-done | bytes 262168
  5.2 0.0 copy-start.3
  5.2 0.9 %copy-done.3 = bf16[8,4,2048]{2,1,0:T(4,128)(2,1)S(1)} copy-done((bf16[8,4,2048]{2,1,0:T(4,128)(2,1)S(1)}, bf16[8,4,2048]{2,1,0:T(4,128)(2,1)}, u32[]{:S(2)}) %copy-start.3) | copy-done | bytes 131096
  6.1 0.0 copy-start.4
  6.1 0.8 %copy-done.4 = bf16[64,4,128]{2,1,0:T(4,128)(2,1)S(1)} copy-done((bf16[64,4,128]{2,1,0:T(4,128)(2,1)S(1)}, bf16[64,4,128]{2,1,0:T(4,128)(2,1)}, u32[]{:S(2)}) %copy-start.4) | copy-done | bytes 65560
  7.0 0.0 copy-start.5
  7.0 0.7 %copy-done.5 = f32[2048]{0:T(1024)S(1)} copy-done((f32[2048]{0:T(1024)S(1)}, f32[2048]{0:T(1024)}, u32[]{:S(2)}) %copy-start.5) | copy-done | bytes 8216
  7.7 0.0 copy-start.6
  7.7 0.7 %copy-done.6 = s32[64]{0:T(128)S(1)} copy-done((s32[64]{0:T(128)S(1)}, s32[64]{0:T(128)}, u32[]{:S(2)}) %copy-start.6) | copy-done | bytes 280
  8.3 0.0 copy-start.7
  8.3 0.7 %copy-done.7 = s32[128]{0:T(128)S(1)} copy-done((s32[128]{0:T(128)S(1)}, s32[128]{0:T(128)}, u32[]{:S(2)}) %copy-start.7) | copy-done | bytes 536
  9.0 46.6 %shard_map.131 = (bf16[128,1024]{1,0:T(8,128)(2,1)S(1)}, bf16[128,1024]{1,0:T(8,128)(2,1)S(1)}) custom-call(bf16[64,4,128]{2,1,0:T(4,128)(2,1)S(1)} %copy-done.4, s32[1,64]{1,0:T(1,128)S(1)} %bitcast.6, bf16[64,2048]{1,0:T(8,128)(2,1)S(1)} %copy-done.2, bf16[8,4,2048]{2,1,0:T(4,128)(2,1)S(1)} %copy-done.3, f32[1,2048]{1,0:T(1,128)S(1)} %bitcast.4, ...), custom_call_target="tpu_custom_call" | custom-call | tf_op jit(solution)/shard_map/pallas_call | solution.py:391
  55.6 0.7 %copy.16 = bf16[128,1024]{1,0:T(8,128)(2,1)} copy(bf16[128,1024]{1,0:T(8,128)(2,1)S(1)} %get-tuple-element.4) | data formatting | bytes 524288
  56.3 0.7 %copy.17 = bf16[128,1024]{1,0:T(8,128)(2,1)} copy(bf16[128,1024]{1,0:T(8,128)(2,1)S(1)} %get-tuple-element.5) | data formatting | bytes 524288
Async XLA Ops:
  1.3 1.6 %copy-start = (bf16[2048,512]{1,0:T(8,128)(2,1)S(1)}, bf16[2048,512]{1,0:T(8,128)(2,1)}, u32[]{:S(2)}) copy-start(bf16[2048,512]{1,0:T(8,128)(2,1)} %wq_ref.1) | copy-start | bytes 6291460
  2.9 1.4 %copy-start.1 = (bf16[360,2048]{1,0:T(8,128)(2,1)S(1)}, bf16[360,2048]{1,0:T(8,128)(2,1)}, u32[]{:S(2)}) copy-start(bf16[360,2048]{1,0:T(8,128)(2,1)} %lat_ref.1) | copy-start | bytes 4423684
  4.3 0.9 %copy-start.2 = (bf16[64,2048]{1,0:T(8,128)(2,1)S(1)}, bf16[64,2048]{1,0:T(8,128)(2,1)}, u32[]{:S(2)}) copy-start(bf16[64,2048]{1,0:T(8,128)(2,1)} %emb_ref.1) | copy-start | bytes 786436
  5.2 0.9 %copy-start.3 = (bf16[8,4,2048]{2,1,0:T(4,128)(2,1)S(1)}, bf16[8,4,2048]{2,1,0:T(4,128)(2,1)}, u32[]{:S(2)}) copy-start(bf16[8,4,2048]{2,1,0:T(4,128)(2,1)} %gw_ref.1) | copy-start | bytes 393220
  6.1 0.8 %copy-start.4 = (bf16[64,4,128]{2,1,0:T(4,128)(2,1)S(1)}, bf16[64,4,128]{2,1,0:T(4,128)(2,1)}, u32[]{:S(2)}) copy-start(bf16[64,4,128]{2,1,0:T(4,128)(2,1)} %pix_ref.1) | copy-start | bytes 196612
  7.0 0.7 %copy-start.5 = (f32[2048]{0:T(1024)S(1)}, f32[2048]{0:T(1024)}, u32[]{:S(2)}) copy-start(f32[2048]{0:T(1024)} %param.19) | copy-start | bytes 24580
  7.7 0.7 %copy-start.6 = (s32[64]{0:T(128)S(1)}, s32[64]{0:T(128)}, u32[]{:S(2)}) copy-start(s32[64]{0:T(128)} %param.13) | copy-start | bytes 772
  8.3 0.7 %copy-start.7 = (s32[128]{0:T(128)S(1)}, s32[128]{0:T(128)}, u32[]{:S(2)}) copy-start(s32[128]{0:T(128)} %param.17) | copy-start | bytes 1540

commit v2 on v1

--- a/solution.py
+++ b/solution.py
@@ -16,11 +16,12 @@
 
 def kernel(
     S, R, C,
-    pix_ref, vg_ref, emb_ref, gw_ref, q_ref, lidx_ref, lat_ref, gain_ref,
+    pix_hbm, vg_hbm, emb_ref, gw_hbm, q_hbm, lidx_hbm, lat_ref, gain_hbm,
     wq_ref, wk_ref, wv_ref, wo_ref,
     agg_ref, att_ref,
+    pix_ref, vg_ref, gw_ref, q_ref, lidx_ref, gain_ref,
     bm, latv, wqv, wkv, wvv, woa, gtmp, pixf, cf, ck, lt, nm, kv, qs, ms, ls, acc, ho,
-    loc, e_s, e_r, ep_s, ep_r, c_s, c_r, o_s, o_r, op_s, op_r, h_s, h_r, k_s, k_r,
+    loc, e_s, e_r, ep_s, ep_r, c_s, c_r, o_s, o_r, op_s, op_r, h_s, h_r, y_s, y_r, k_s, k_r,
 ):
     D = emb_ref.shape[1]
     Vl = emb_ref.shape[0]
@@ -33,7 +34,8 @@
     share = D // S
     half = D // 2
     clh = Cl // 2
-    Kp = ck.shape[0]
+    Kp = ck.shape[1]
+    used = S * Vl + GP
     W = C * 2 * T
     s = lax.axis_index("segment")
     b = lax.axis_index("blk")
@@ -56,10 +58,19 @@
     greet(s, partner)
     pl.when(r > 0)(lambda: greet(s, b - 2 * C))
     pl.when(r < R - 1)(lambda: greet(s, b + 2 * C))
-    pl.when(col > 0)(lambda: greet(s, b - 2))
-    pl.when(col < C - 1)(lambda: greet(s, b + 2))
+    for k in range(1, C):
+        greet(s, b + 2 * (lax.rem(col + k, C) - col))
 
     own_rows = pl.ds(pl.multiple_of(s * Vl, Vl), Vl)
+    small = [
+        pltpu.make_async_copy(src, dst, loc.at[6 + i])
+        for i, (src, dst) in enumerate(
+            [(gw_hbm, gw_ref), (q_hbm, q_ref), (pix_hbm, pix_ref), (vg_hbm, vg_ref),
+             (lidx_hbm, lidx_ref), (gain_hbm, gain_ref)]
+        )
+    ]
+    for one in small[:2]:
+        one.start()
     locals_ = [
         pltpu.make_async_copy(emb_ref, bm.at[own_rows], loc.at[0]),
         pltpu.make_async_copy(lat_ref, latv, loc.at[1]),
@@ -70,14 +81,15 @@
             wo_ref.at[:, pl.ds(pl.multiple_of(s * share, share), share)], woa.at[s], loc.at[5]
         ),
     ]
-    for one in locals_:
+    locals_[0].start()
+    for one in small[2:] + locals_[1:]:
         one.start()
     count = (
         S
+        + C
+        - 1
         + jnp.minimum(r, 1)
         + jnp.minimum(R - 1 - r, 1)
-        + jnp.minimum(col, 1)
-        + jnp.minimum(C - 1 - col, 1)
     )
     pl.semaphore_wait(barrier, count)
 
@@ -103,7 +115,9 @@
     for one in e_out:
         one.start()
 
+    small[1].wait()
     q = q_ref[...]
+    small[0].wait()
     for g in range(G):
         one_group = gw_ref[g].astype(F32)
         for p in range(PX):
@@ -113,8 +127,10 @@
     if Kp > S * Vl + GP:
         bm[S * Vl + GP : Kp, :] = jnp.zeros((Kp - S * Vl - GP, D), BF16)
     pg = jnp.sum(gwp * q, axis=1, keepdims=True)
+    small[2].wait()
     for v in range(Vl):
         pixf[PX * v : PX * v + PX, :] = pix_ref[v].astype(F32)
+    small[3].wait()
     vg = vg_ref[...]
     row_at = lax.broadcasted_iota(jnp.int32, (Vl, Vl), 0)
     col_at = lax.broadcasted_iota(jnp.int32, (Vl, Vl), 1)
@@ -158,9 +174,11 @@
     for one in o_out:
         one.start()
 
-    lat_rows = ((NL + 127) // 128) * 128
-    hot = (lax.broadcasted_iota(jnp.int32, (lat_rows, T), 0) == lidx_ref[...]).astype(F32)
-    hot = hot.T.astype(BF16)[:, :NL]
+    small[4].wait()
+    ck[col, used : used + 8, :] = jnp.broadcast_to(lidx_ref[...].astype(F32), (8, T))
+    if Kp > used + 8:
+        for c0 in range(C):
+            ck[c0, used + 8 : Kp, :] = jnp.zeros((Kp - used - 8, T), F32)
 
     ep_out = []
     for k in range(1, S):
@@ -184,41 +202,17 @@
     grouped = jnp.zeros((GP, T), F32)
     for k in range(S):
         share_k = factors[k] / total
-        ck[k * Vl : k * Vl + Vl, :] = cf[k, 0:Vl, :] * share_k
+        ck[col, k * Vl : k * Vl + Vl, :] = cf[k, 0:Vl, :] * share_k
         grouped = grouped + cf[k, Vl : Vl + GP, :] * share_k
-    ck[S * Vl : S * Vl + GP, :] = grouped
-    if Kp > S * Vl + GP:
-        ck[S * Vl + GP : Kp, :] = jnp.zeros((Kp - S * Vl - GP, T), F32)
-    ct = ck[...].T
-    hi = ct.astype(BF16)
-    rest = ct - hi.astype(F32)
-    mid = rest.astype(BF16)
-    low = (rest - mid.astype(F32)).astype(BF16)
-    for k in range(1, S):
-        src = seg_at(S - k)
-        other = emb_region(src, 1 - c)
-        remote(other, other, ep_s.at[k], ep_r.at[k], s, partner).wait_recv()
-    locals_[1].wait()
-    step = 512
-    mean = jnp.zeros((T, 1), F32)
-    for j in range(D // step):
-        at = slice(j * step, (j + 1) * step)
-        base = bm[:, at]
-        part = jnp.dot(low, base, preferred_element_type=F32)
-        part = part + jnp.dot(mid, base, preferred_element_type=F32)
-        part = part + jnp.dot(hi, base, preferred_element_type=F32)
-        part = part + jnp.dot(hot, latv[:, at], preferred_element_type=F32)
-        lt[:, at] = part
-        mean = mean + jnp.sum(part, axis=1, keepdims=True)
-    mean = mean / D
-    spread = jnp.zeros((T, 1), F32)
-    for j in range(D // step):
-        center = lt[:, j * step : (j + 1) * step] - mean
-        spread = spread + jnp.sum(center * center, axis=1, keepdims=True)
-    inv = lax.rsqrt(spread / D + 1e-05)
-    for j in range(D // step):
-        at = slice(j * step, (j + 1) * step)
-        nm[:, at] = ((lt[:, at] - mean) * inv * gain_ref[:, at]).astype(BF16)
+    ck[col, S * Vl : used, :] = grouped
+    y_out = []
+    for k in range(1, C):
+        to = lax.rem(col + k, C)
+        block = ck.at[col, pl.ds(0, used + 8)]
+        one = remote(block, block, y_s.at[k], y_r.at[k], s, b + 2 * (to - col))
+        one.start()
+        y_out.append(one)
+    small[5].wait()
 
     def region(part, blk):
         return kv.at[part, pl.ds(pl.multiple_of(blk * T, T), T)]
@@ -236,8 +230,8 @@
         def go(part):
             pl.when(here & (r > 0) & (r0 >= r))(lambda: act(each(part, 0, b - 2 * C)))
             pl.when(here & (r < R - 1) & (r0 <= r))(lambda: act(each(part, 1, b + 2 * C)))
-            pl.when((col > 0) & (c0 >= col))(lambda: act(each(part, 2, b - 2)))
-            pl.when((col < C - 1) & (c0 <= col))(lambda: act(each(part, 3, b + 2)))
+            pl.when((r0 != r) & (col > 0) & (c0 >= col))(lambda: act(each(part, 2, b - 2)))
+            pl.when((r0 != r) & (col < C - 1) & (c0 <= col))(lambda: act(each(part, 3, b + 2)))
             act(each(part, 4, partner))
 
         return go
@@ -251,17 +245,73 @@
             s, partner,
         ).wait_recv()
 
-    mine = sends(r, col, start)
-    own_keys = pl.ds(pl.multiple_of(b * T, T), T)
-    locals_[2].wait()
-    kv[0, own_keys, :] = jnp.dot(nm[...], wkv[...], preferred_element_type=F32).astype(BF16)
-    mine(0)
-    locals_[3].wait()
-    kv[1, own_keys, :] = jnp.dot(nm[...], wvv[...], preferred_element_type=F32).astype(BF16)
-    mine(1)
-    locals_[4].wait()
-    qs[...] = jnp.dot(nm[...], wqv[...], preferred_element_type=F32).astype(BF16)
-    agg_ref[...] = lt[:, pl.ds(pl.multiple_of(s * share, share), share)].astype(BF16)
+    lat_rows = ((NL + 127) // 128) * 128
+    step = 512
+
+    def own_block(turn, carry):
+        c0 = lax.rem(col + turn, C)
+
+        @pl.when(turn > 0)
+        def _():
+            block = ck.at[c0, pl.ds(0, used + 8)]
+            back = C - turn
+            remote(block, block, y_s.at[back], y_r.at[back], s, partner).wait_recv()
+
+        ct = ck[c0].T
+        hi = ct.astype(BF16)
+        rest = ct - hi.astype(F32)
+        mid = rest.astype(BF16)
+        low = (rest - mid.astype(F32)).astype(BF16)
+        at_row = ck[c0, used : used + 1, :]
+        rows = lax.broadcasted_iota(jnp.int32, (lat_rows, T), 0).astype(F32)
+        hot = (rows == at_row).astype(F32).T.astype(BF16)[:, :NL]
+
+        @pl.when(turn == 0)
+        def _():
+            for k in range(1, S):
+                other = emb_region(seg_at(S - k), 1 - c)
+                remote(other, other, ep_s.at[k], ep_r.at[k], s, partner).wait_recv()
+            locals_[1].wait()
+
+        mean = jnp.zeros((T, 1), F32)
+        for j in range(D // step):
+            at = slice(j * step, (j + 1) * step)
+            base = bm[:, at]
+            part = jnp.dot(low, base, preferred_element_type=F32)
+            part = part + jnp.dot(mid, base, preferred_element_type=F32)
+            part = part + jnp.dot(hi, base, preferred_element_type=F32)
+            part = part + jnp.dot(hot, latv[:, at], preferred_element_type=F32)
+            lt[:, at] = part
+            mean = mean + jnp.sum(part, axis=1, keepdims=True)
+        mean = mean / D
+        spread = jnp.zeros((T, 1), F32)
+        for j in range(D // step):
+            center = lt[:, j * step : (j + 1) * step] - mean
+            spread = spread + jnp.sum(center * center, axis=1, keepdims=True)
+        inv = lax.rsqrt(spread / D + 1e-05)
+        for j in range(D // step):
+            at = slice(j * step, (j + 1) * step)
+            nm[:, at] = ((lt[:, at] - mean) * inv * gain_ref[:, at]).astype(BF16)
+
+        blk = (r * C + c0) * 2 + c
+        keys_at = pl.ds(pl.multiple_of(blk * T, T), T)
+        ready = sends(r, c0, start)
+        pl.when(turn == 0)(lambda: locals_[2].wait())
+        kv[0, keys_at, :] = jnp.dot(nm[...], wkv[...], preferred_element_type=F32).astype(BF16)
+        ready(0)
+        pl.when(turn == 0)(lambda: locals_[3].wait())
+        kv[1, keys_at, :] = jnp.dot(nm[...], wvv[...], preferred_element_type=F32).astype(BF16)
+        ready(1)
+
+        @pl.when(turn == 0)
+        def _():
+            locals_[4].wait()
+            qs[...] = jnp.dot(nm[...], wqv[...], preferred_element_type=F32).astype(BF16)
+            agg_ref[...] = lt[:, pl.ds(pl.multiple_of(s * share, share), share)].astype(BF16)
+
+        return carry
+
+    lax.fori_loop(0, C, own_block, 0)
     ms[...] = jnp.full(ms.shape, -1e30, F32)
     ls[...] = jnp.zeros(ls.shape, F32)
     acc[...] = jnp.zeros(acc.shape, F32)
@@ -298,7 +348,7 @@
             for way in (-1, 1):
                 c0 = col + way * dist
 
-                @pl.when((c0 >= 0) & (c0 < C))
+                @pl.when((row != r) & (c0 >= 0) & (c0 < C))
                 def _():
                     for part in range(2):
                         arrived(part, (row * C + c0) * 2 + c)
@@ -351,7 +401,7 @@
         lt[:, 0:share] = lt[:, 0:share] + jnp.dot(ho[src], woa[src], preferred_element_type=F32)
     att_ref[...] = lt[:, 0:share].astype(BF16)
 
-    for one in e_out + ep_out + c_out + o_out + op_out + h_out:
+    for one in e_out + ep_out + c_out + y_out + o_out + op_out + h_out:
         one.wait_send()
 
     def drain(i, carry):
@@ -383,17 +433,23 @@
         cl = w_query.shape[1]
         H = cl // HEAD_DIM
         share = D // S
-        kp = ((S * vl + G * PX + 127) // 128) * 128
+        kp = ((S * vl + G * PX + 8 + 127) // 128) * 128
         vm = pl.BlockSpec(memory_space=pltpu.VMEM)
-        far = pl.BlockSpec(memory_space=pl.ANY)
+        far = pl.BlockSpec(memory_space=pltpu.HBM)
         dma = pltpu.SemaphoreType.DMA
         out = jax.ShapeDtypeStruct((T, share), BF16)
         return pl.pallas_call(
             functools.partial(kernel, S, R, C),
             out_shape=(out, out),
-            in_specs=[vm, vm, far, vm, vm, vm, far, vm, far, far, far, far],
+            in_specs=[far] * 12,
             out_specs=(vm, vm),
             scratch_shapes=[
+                pltpu.VMEM((vl, PX, T), BF16),
+                pltpu.VMEM((1, vl), jnp.int32),
+                pltpu.VMEM((G, PX, D), BF16),
+                pltpu.VMEM((1, D), F32),
+                pltpu.VMEM((1, T), jnp.int32),
+                pltpu.VMEM((1, D), F32),
                 pltpu.VMEM((kp, D), BF16),
                 pltpu.VMEM((NL, D), BF16),
                 pltpu.VMEM((D, cl), BF16),
@@ -403,7 +459,7 @@
                 pltpu.VMEM((G * PX, D), F32),
                 pltpu.VMEM((vl * PX, T), F32),
                 pltpu.VMEM((S, vl + G * PX + 16, T), F32),
-                pltpu.VMEM((kp, T), F32),
+                pltpu.VMEM((C, kp, T), F32),
                 pltpu.VMEM((T, D), F32),
                 pltpu.VMEM((T, D), BF16),
                 pltpu.VMEM((2, B * T, cl), BF16),
@@ -412,10 +468,10 @@
                 pltpu.VMEM((H, T, 128), F32),
                 pltpu.VMEM((T, cl), F32),
                 pltpu.VMEM((S, T, cl), BF16),
-                dma((6,)),
+                dma((12,)),
             ]
             + [dma((S,))] * 12
-            + [dma((5, 2, B)), dma((2, B))],
+            + [dma((C,)), dma((C,)), dma((5, 2, B)), dma((2, B))],
             compiler_params=pltpu.CompilerParams(
                 collective_id=0, has_side_effects=True, vmem_limit_bytes=48 * 1024 * 1024
             ),

time: 57.3 us -> 59.4 us (1.037)
  Pallas kernels: 46.6 us -> 48.7 us
    pallas_call x1, Pallas kernels: 46.6 us -> 48.7 us  [on_device(): pl.pallas_call(functools.partial(kernel, S, R, C), out_shape=(out, out),...]
where the time goes in v2:
time: 59.4 us; the launch traced here: 59.1 us
  Pallas kernels  48.7 us (82%)
  local copies, waits for them, and re-layouts  9.07 us (15%)
  other arithmetic  0.69 us (1%)
  between operations  0.65 us (1%)
    pallas_call x1, Pallas kernels, on_device(): pl.pallas_call(functools.partial(kernel, S, R, C), out_shape=(out, out),...  48.7 us
    unnamed x18, local copies, waits for them, and re-layouts  9.07 us

profile of v2, /device:TPU:0, one launch (start us, length us, event | category | flops | bytes accessed | tf_op | source)
XLA Modules:
  0.0 59.1 jit_solution(16535508498342597898)
XLA Ops:
  0.6 0.7 %reshape.23 = f32[2048]{0:T(1024)S(1)} convert(bf16[2048]{0:T(1024)(128)(2,1)} %param.16) | non-fusion elementwise | flops 2048 | bytes 12288 | tf_op jit(solution)/shard_map/reshape | solution.py:483
  1.3 0.0 copy-start
  1.3 1.6 %copy-done = bf16[2048,512]{1,0:T(8,128)(2,1)S(1)} copy-done((bf16[2048,512]{1,0:T(8,128)(2,1)S(1)}, bf16[2048,512]{1,0:T(8,128)(2,1)}, u32[]{:S(2)}) %copy-start) | copy-done | bytes 2097176
  2.9 0.0 copy-start.1
  2.9 1.4 %copy-done.1 = bf16[360,2048]{1,0:T(8,128)(2,1)S(1)} copy-done((bf16[360,2048]{1,0:T(8,128)(2,1)S(1)}, bf16[360,2048]{1,0:T(8,128)(2,1)}, u32[]{:S(2)}) %copy-start.1) | copy-done | bytes 1474584
  4.3 0.0 copy-start.2
  4.3 0.9 %copy-done.2 = bf16[64,2048]{1,0:T(8,128)(2,1)S(1)} copy-done((bf16[64,2048]{1,0:T(8,128)(2,1)S(1)}, bf16[64,2048]{1,0:T(8,128)(2,1)}, u32[]{:S(2)}) %copy-start.2) | copy-done | bytes 262168
  5.2 0.0 copy-start.3
  5.2 0.9 %copy-done.3 = bf16[8,4,2048]{2,1,0:T(4,128)(2,1)S(1)} copy-done((bf16[8,4,2048]{2,1,0:T(4,128)(2,1)S(1)}, bf16[8,4,2048]{2,1,0:T(4,128)(2,1)}, u32[]{:S(2)}) %copy-start.3) | copy-done | bytes 131096
  6.1 0.0 copy-start.4
  6.1 0.8 %copy-done.4 = bf16[64,4,128]{2,1,0:T(4,128)(2,1)S(1)} copy-done((bf16[64,4,128]{2,1,0:T(4,128)(2,1)S(1)}, bf16[64,4,128]{2,1,0:T(4,128)(2,1)}, u32[]{:S(2)}) %copy-start.4) | copy-done | bytes 65560
  7.0 0.0 copy-start.5
  7.0 0.7 %copy-done.5 = f32[2048]{0:T(1024)S(1)} copy-done((f32[2048]{0:T(1024)S(1)}, f32[2048]{0:T(1024)}, u32[]{:S(2)}) %copy-start.5) | copy-done | bytes 8216
  7.7 0.0 copy-start.6
  7.7 0.7 %copy-done.6 = s32[64]{0:T(128)S(1)} copy-done((s32[64]{0:T(128)S(1)}, s32[64]{0:T(128)}, u32[]{:S(2)}) %copy-start.6) | copy-done | bytes 280
  8.3 0.0 copy-start.7
  8.3 0.7 %copy-done.7 = s32[128]{0:T(128)S(1)} copy-done((s32[128]{0:T(128)S(1)}, s32[128]{0:T(128)}, u32[]{:S(2)}) %copy-start.7) | copy-done | bytes 536
  9.0 48.7 %shard_map.131 = (bf16[128,1024]{1,0:T(8,128)(2,1)S(1)}, bf16[128,1024]{1,0:T(8,128)(2,1)S(1)}) custom-call(bf16[64,4,128]{2,1,0:T(4,128)(2,1)S(1)} %copy-done.4, s32[1,64]{1,0:T(1,128)S(1)} %bitcast.6, bf16[64,2048]{1,0:T(8,128)(2,1)S(1)} %copy-done.2, bf16[8,4,2048]{2,1,0:T(4,128)(2,1)S(1)} %copy-done.3, f32[1,2048]{1,0:T(1,128)S(1)} %bitcast.4, ...), custom_call_target="tpu_custom_call" | custom-call | tf_op jit(solution)/shard_map/pallas_call | solution.py:441
  57.7 0.7 %copy.16 = bf16[128,1024]{1,0:T(8,128)(2,1)} copy(bf16[128,1024]{1,0:T(8,128)(2,1)S(1)} %get-tuple-element.4) | data formatting | bytes 524288
  58.4 0.7 %copy.17 = bf16[128,1024]{1,0:T(8,128)(2,1)} copy(bf16[128,1024]{1,0:T(8,128)(2,1)S(1)} %get-tuple-element.5) | data formatting | bytes 524288
Async XLA Ops:
  1.3 1.6 %copy-start = (bf16[2048,512]{1,0:T(8,128)(2,1)S(1)}, bf16[2048,512]{1,0:T(8,128)(2,1)}, u32[]{:S(2)}) copy-start(bf16[2048,512]{1,0:T(8,128)(2,1)} %wq_ref.1) | copy-start | bytes 6291460
  2.9 1.4 %copy-start.1 = (bf16[360,2048]{1,0:T(8,128)(2,1)S(1)}, bf16[360,2048]{1,0:T(8,128)(2,1)}, u32[]{:S(2)}) copy-start(bf16[360,2048]{1,0:T(8,128)(2,1)} %lat_ref.1) | copy-start | bytes 4423684
  4.3 0.9 %copy-start.2 = (bf16[64,2048]{1,0:T(8,128)(2,1)S(1)}, bf16[64,2048]{1,0:T(8,128)(2,1)}, u32[]{:S(2)}) copy-start(bf16[64,2048]{1,0:T(8,128)(2,1)} %emb_ref.1) | copy-start | bytes 786436
  5.2 0.9 %copy-start.3 = (bf16[8,4,2048]{2,1,0:T(4,128)(2,1)S(1)}, bf16[8,4,2048]{2,1,0:T(4,128)(2,1)}, u32[]{:S(2)}) copy-start(bf16[8,4,2048]{2,1,0:T(4,128)(2,1)} %gw_hbm.1) | copy-start | bytes 393220
  6.1 0.8 %copy-start.4 = (bf16[64,4,128]{2,1,0:T(4,128)(2,1)S(1)}, bf16[64,4,128]{2,1,0:T(4,128)(2,1)}, u32[]{:S(2)}) copy-start(bf16[64,4,128]{2,1,0:T(4,128)(2,1)} %pix_hbm.1) | copy-start | bytes 196612
  7.0 0.7 %copy-start.5 = (f32[2048]{0:T(1024)S(1)}, f32[2048]{0:T(1024)}, u32[]{:S(2)}) copy-start(f32[2048]{0:T(1024)} %param.19) | copy-start | bytes 24580
  7.7 0.7 %copy-start.6 = (s32[64]{0:T(128)S(1)}, s32[64]{0:T(128)}, u32[]{:S(2)}) copy-start(s32[64]{0:T(128)} %param.13) | copy-start | bytes 772
  8.3 0.7 %copy-start.7 = (s32[128]{0:T(128)S(1)}, s32[128]{0:T(128)}, u32[]{:S(2)}) copy-start(s32[128]{0:T(128)} %param.17) | copy-start | bytes 1540

commit v3 on v2

--- a/solution.py
+++ b/solution.py
@@ -56,10 +56,13 @@
     for k in range(1, S):
         greet(lax.rem(s + k, S), b)
     greet(s, partner)
-    pl.when(r > 0)(lambda: greet(s, b - 2 * C))
-    pl.when(r < R - 1)(lambda: greet(s, b + 2 * C))
-    for k in range(1, C):
-        greet(s, b + 2 * (lax.rem(col + k, C) - col))
+    chips = R * C
+
+    def greet_chip(k, carry):
+        greet(s, lax.rem(rc + k, chips) * 2 + c)
+        return carry
+
+    lax.fori_loop(1, chips, greet_chip, 0)
 
     own_rows = pl.ds(pl.multiple_of(s * Vl, Vl), Vl)
     small = [
@@ -84,13 +87,7 @@
     locals_[0].start()
     for one in small[2:] + locals_[1:]:
         one.start()
-    count = (
-        S
-        + C
-        - 1
-        + jnp.minimum(r, 1)
-        + jnp.minimum(R - 1 - r, 1)
-    )
+    count = S + chips - 1
     pl.semaphore_wait(barrier, count)
 
     def remote(src, dst, send, recv, seg, blk):
@@ -175,10 +172,14 @@
         one.start()
 
     small[4].wait()
-    ck[col, used : used + 8, :] = jnp.broadcast_to(lidx_ref[...].astype(F32), (8, T))
+    ck[rc, used : used + 8, :] = jnp.broadcast_to(lidx_ref[...].astype(F32), (8, T))
     if Kp > used + 8:
-        for c0 in range(C):
-            ck[c0, used + 8 : Kp, :] = jnp.zeros((Kp - used - 8, T), F32)
+
+        def clear(i, carry):
+            ck[i, used + 8 : Kp, :] = jnp.zeros((Kp - used - 8, T), F32)
+            return carry
+
+        lax.fori_loop(0, chips, clear, 0)
 
     ep_out = []
     for k in range(1, S):
@@ -202,78 +203,79 @@
     grouped = jnp.zeros((GP, T), F32)
     for k in range(S):
         share_k = factors[k] / total
-        ck[col, k * Vl : k * Vl + Vl, :] = cf[k, 0:Vl, :] * share_k
+        ck[rc, k * Vl : k * Vl + Vl, :] = cf[k, 0:Vl, :] * share_k
         grouped = grouped + cf[k, Vl : Vl + GP, :] * share_k
-    ck[col, S * Vl : used, :] = grouped
-    y_out = []
-    for k in range(1, C):
-        to = lax.rem(col + k, C)
-        block = ck.at[col, pl.ds(0, used + 8)]
-        one = remote(block, block, y_s.at[k], y_r.at[k], s, b + 2 * (to - col))
-        one.start()
-        y_out.append(one)
+    ck[rc, S * Vl : used, :] = grouped
+    mine = ck.at[rc, pl.ds(0, used + 8)]
+
+    def spread_to(dist, row_way, act):
+        row = r + (2 * row_way - 1) * dist
+
+        @pl.when((row >= 0) & (row < R) & (dist + row_way > 0))
+        def _():
+            def one_col(k, carry):
+                chip = row * C + lax.rem(col + k, C)
+
+                @pl.when(chip != rc)
+                def _():
+                    act(remote(mine, mine, y_s.at[chip], y_r.at[rc], s, chip * 2 + c))
+
+                return carry
+
+            lax.fori_loop(0, C, one_col, 0)
+
+    def all_chips(act):
+        def outer(i, carry):
+            spread_to(i // 2, lax.rem(i, 2), act)
+            return carry
+
+        lax.fori_loop(0, 2 * R, outer, 0)
+
+    all_chips(lambda copy: copy.start())
     small[5].wait()
 
     def region(part, blk):
         return kv.at[part, pl.ds(pl.multiple_of(blk * T, T), T)]
 
-    def sends(r0, c0, act):
-        blk = (r0 * C + c0) * 2 + c
-        here = c0 == col
-
-        def each(part, way, to):
-            return remote(
-                region(part, blk), region(part, blk), k_s.at[way, part, blk], k_r.at[part, blk],
-                s, to,
-            )
-
-        def go(part):
-            pl.when(here & (r > 0) & (r0 >= r))(lambda: act(each(part, 0, b - 2 * C)))
-            pl.when(here & (r < R - 1) & (r0 <= r))(lambda: act(each(part, 1, b + 2 * C)))
-            pl.when((r0 != r) & (col > 0) & (c0 >= col))(lambda: act(each(part, 2, b - 2)))
-            pl.when((r0 != r) & (col < C - 1) & (c0 <= col))(lambda: act(each(part, 3, b + 2)))
-            act(each(part, 4, partner))
-
-        return go
-
-    def start(copy):
-        copy.start()
-
-    def arrived(part, blk):
-        remote(
-            region(part, blk), region(part, blk), k_s.at[4, part, blk], k_r.at[part, blk],
+    def shared(part, blk):
+        return remote(
+            region(part, blk), region(part, blk), k_s.at[part, blk], k_r.at[part, blk],
             s, partner,
-        ).wait_recv()
+        )
 
     lat_rows = ((NL + 127) // 128) * 128
-    step = 512
-
-    def own_block(turn, carry):
-        c0 = lax.rem(col + turn, C)
-
-        @pl.when(turn > 0)
-        def _():
-            block = ck.at[c0, pl.ds(0, used + 8)]
-            back = C - turn
-            remote(block, block, y_s.at[back], y_r.at[back], s, partner).wait_recv()
-
-        ct = ck[c0].T
-        hi = ct.astype(BF16)
-        rest = ct - hi.astype(F32)
+    step = 256
+
+    def pieces(x):
+        hi = x.astype(BF16)
+        rest = x - hi.astype(F32)
         mid = rest.astype(BF16)
-        low = (rest - mid.astype(F32)).astype(BF16)
-        at_row = ck[c0, used : used + 1, :]
-        rows = lax.broadcasted_iota(jnp.int32, (lat_rows, T), 0).astype(F32)
-        hot = (rows == at_row).astype(F32).T.astype(BF16)[:, :NL]
-
-        @pl.when(turn == 0)
+        return hi, mid, (rest - mid.astype(F32)).astype(BF16)
+
+    def compute(row, first):
+        split = []
+        for c0 in range(C):
+            chip = row * C + c0
+
+            @pl.when(chip != rc)
+            def _():
+                there = ck.at[chip, pl.ds(0, used + 8)]
+                remote(there, there, y_s.at[chip], y_r.at[chip], s, partner).wait_recv()
+
+            at_row = ck[chip, used : used + 1, :]
+            rows = lax.broadcasted_iota(jnp.int32, (lat_rows, T), 0).astype(F32)
+            hot = (rows == at_row).astype(F32).T.astype(BF16)[:, :NL]
+            split.append(pieces(ck[chip].T) + (hot,))
+        hi, mid, low, hot = [jnp.concatenate(x, axis=0) for x in zip(*split)]
+
+        @pl.when(first)
         def _():
             for k in range(1, S):
                 other = emb_region(seg_at(S - k), 1 - c)
                 remote(other, other, ep_s.at[k], ep_r.at[k], s, partner).wait_recv()
             locals_[1].wait()
 
-        mean = jnp.zeros((T, 1), F32)
+        mean = jnp.zeros((C * T, 1), F32)
         for j in range(D // step):
             at = slice(j * step, (j + 1) * step)
             base = bm[:, at]
@@ -284,7 +286,7 @@
             lt[:, at] = part
             mean = mean + jnp.sum(part, axis=1, keepdims=True)
         mean = mean / D
-        spread = jnp.zeros((T, 1), F32)
+        spread = jnp.zeros((C * T, 1), F32)
         for j in range(D // step):
             center = lt[:, j * step : (j + 1) * step] - mean
             spread = spread + jnp.sum(center * center, axis=1, keepdims=True)
@@ -292,26 +294,21 @@
         for j in range(D // step):
             at = slice(j * step, (j + 1) * step)
             nm[:, at] = ((lt[:, at] - mean) * inv * gain_ref[:, at]).astype(BF16)
-
-        blk = (r * C + c0) * 2 + c
-        keys_at = pl.ds(pl.multiple_of(blk * T, T), T)
-        ready = sends(r, c0, start)
-        pl.when(turn == 0)(lambda: locals_[2].wait())
-        kv[0, keys_at, :] = jnp.dot(nm[...], wkv[...], preferred_element_type=F32).astype(BF16)
-        ready(0)
-        pl.when(turn == 0)(lambda: locals_[3].wait())
-        kv[1, keys_at, :] = jnp.dot(nm[...], wvv[...], preferred_element_type=F32).astype(BF16)
-        ready(1)
-
-        @pl.when(turn == 0)
+        for part, weight in ((0, wkv), (1, wvv)):
+            pl.when(first)(lambda: locals_[2 + part].wait())
+            made = jnp.dot(nm[...], weight[...], preferred_element_type=F32).astype(BF16)
+            for c0 in range(C):
+                blk = (row * C + c0) * 2 + c
+                kv[part, pl.ds(pl.multiple_of(blk * T, T), T), :] = made[c0 * T : (c0 + 1) * T]
+                shared(part, blk).start()
+
+        @pl.when(first)
         def _():
             locals_[4].wait()
-            qs[...] = jnp.dot(nm[...], wqv[...], preferred_element_type=F32).astype(BF16)
-            agg_ref[...] = lt[:, pl.ds(pl.multiple_of(s * share, share), share)].astype(BF16)
-
-        return carry
-
-    lax.fori_loop(0, C, own_block, 0)
+            own = pl.ds(pl.multiple_of(col * T, T), T)
+            qs[...] = jnp.dot(nm[own, :], wqv[...], preferred_element_type=F32).astype(BF16)
+            agg_ref[...] = lt[own, pl.ds(pl.multiple_of(s * share, share), share)].astype(BF16)
+
     ms[...] = jnp.full(ms.shape, -1e30, F32)
     ls[...] = jnp.zeros(ls.shape, F32)
     acc[...] = jnp.zeros(acc.shape, F32)
@@ -338,44 +335,25 @@
                 expo.astype(BF16), kv[1, keys_at, cols], preferred_element_type=F32
             )
 
-    def from_column(row):
-        for part in range(2):
-            arrived(part, (row * C + col) * 2 + c)
-            sends(row, col, start)(part)
-
     def finish(row):
-        for dist in range(1, C):
-            for way in (-1, 1):
-                c0 = col + way * dist
-
-                @pl.when((row != r) & (c0 >= 0) & (c0 < C))
-                def _():
-                    for part in range(2):
-                        arrived(part, (row * C + c0) * 2 + c)
-                        sends(row, c0, start)(part)
-
         for c0 in range(C):
             for part in range(2):
-                arrived(part, (row * C + c0) * 2 + 1 - c)
+                shared(part, (row * C + c0) * 2 + 1 - c).wait_recv()
         attend(row)
 
-    def stage(d, carry):
-        def ahead(way, inner):
-            row = r + (2 * way - 1) * (d + 1)
-            pl.when((row >= 0) & (row < R))(lambda: from_column(row))
-            return inner
-
-        lax.fori_loop(0, 2, ahead, 0)
-
-        def now(way, inner):
-            row = r + (2 * way - 1) * d
-            pl.when((row >= 0) & (row < R) & (d + way > 0))(lambda: finish(row))
-            return inner
-
-        lax.fori_loop(0, 2, now, 0)
-        return carry
-
-    lax.fori_loop(0, R, stage, 0)
+    def turn(i, before):
+        dist, way = (i + 1) // 2, lax.rem(i, 2)
+        row = r + (1 - 2 * way) * dist
+        real = (row >= 0) & (row < R)
+
+        @pl.when(real)
+        def _():
+            compute(row, i == 0)
+            pl.when(i > 0)(lambda: finish(before))
+
+        return jnp.where(real, row, before)
+
+    finish(lax.fori_loop(0, 2 * R - 1, turn, r))
 
     for h in range(H):
         cols = slice(h * HEAD_DIM, (h + 1) * HEAD_DIM)
@@ -392,25 +370,26 @@
         one.start()
         op_out.append(one)
     locals_[5].wait()
-    lt[:, 0:share] = jnp.dot(ho[s], woa[s], preferred_element_type=F32)
+    lt[0:T, 0:share] = jnp.dot(ho[s], woa[s], preferred_element_type=F32)
     for k in range(1, S):
         src = seg_at(S - k)
         block = woa.at[src, wo_rows(1 - c)]
         remote(block, block, op_s.at[k], op_r.at[k], s, partner).wait_recv()
         remote(ho.at[src], ho.at[src], h_s.at[k], h_r.at[k], s, partner).wait_recv()
-        lt[:, 0:share] = lt[:, 0:share] + jnp.dot(ho[src], woa[src], preferred_element_type=F32)
-    att_ref[...] = lt[:, 0:share].astype(BF16)
-
-    for one in e_out + ep_out + c_out + y_out + o_out + op_out + h_out:
+        lt[0:T, 0:share] = lt[0:T, 0:share] + jnp.dot(ho[src], woa[src], preferred_element_type=F32)
+    att_ref[...] = lt[0:T, 0:share].astype(BF16)
+
+    for one in e_out + ep_out + c_out + o_out + op_out + h_out:
         one.wait_send()
 
+    all_chips(lambda copy: copy.wait_send())
+
     def drain(i, carry):
-        ends = sends(i // C, lax.rem(i, C), lambda copy: copy.wait_send())
-        ends(0)
-        ends(1)
+        shared(0, i * 2 + c).wait_send()
+        shared(1, i * 2 + c).wait_send()
         return carry
 
-    lax.fori_loop(0, R * C, drain, 0)
+    lax.fori_loop(0, chips, drain, 0)
 
 
 def solution(mesh):
@@ -459,9 +438,9 @@
                 pltpu.VMEM((G * PX, D), F32),
                 pltpu.VMEM((vl * PX, T), F32),
                 pltpu.VMEM((S, vl + G * PX + 16, T), F32),
-                pltpu.VMEM((C, kp, T), F32),
-                pltpu.VMEM((T, D), F32),
-                pltpu.VMEM((T, D), BF16),
+                pltpu.VMEM((chips, kp, T), F32),
+                pltpu.VMEM((C * T, D), F32),
+                pltpu.VMEM((C * T, D), BF16),
                 pltpu.VMEM((2, B * T, cl), BF16),
                 pltpu.VMEM((T, cl), BF16),
                 pltpu.VMEM((H, T, 128), F32),
@@ -471,9 +450,9 @@
                 dma((12,)),
             ]
             + [dma((S,))] * 12
-            + [dma((C,)), dma((C,)), dma((5, 2, B)), dma((2, B))],
+            + [dma((chips,)), dma((chips,)), dma((2, B)), dma((2, B))],
             compiler_params=pltpu.CompilerParams(
-                collective_id=0, has_side_effects=True, vmem_limit_bytes=48 * 1024 * 1024
+                collective_id=0, has_side_effects=True, vmem_limit_bytes=67_043_328
             ),
         )(
             pixels,

time: 59.4 us -> 52.8 us (0.89)
  the two profiles are of different devices: /device:TPU:0 before, /device:TPU:22 now
where the time goes in v3:
time: 52.8 us; the launch traced here: 52.6 us
  Pallas kernels  47.4 us (90%)
  local copies, waits for them, and re-layouts  3.34 us (6%)
  other arithmetic  1.29 us (2%)
  between operations  0.64 us (1%)
    pallas_call x1, Pallas kernels, on_device(): pl.pallas_call(functools.partial(kernel, S, R, C), out_shape=(out, out),...  47.4 us
    unnamed x2, local copies, waits for them, and re-layouts  3.34 us
    reshape x1, other arithmetic, on_device(): agg_query.astype(F32).reshape(1, D)  1.29 us

profile of v3, /device:TPU:22, one launch (start us, length us, event | category | flops | bytes accessed | tf_op | source)
XLA Modules:
  0.0 52.6 jit_solution(5770797114427275710)
XLA Ops:
  0.6 1.3 %reshape.23 = f32[2048]{0:T(1024)} convert(bf16[2048]{0:T(1024)(128)(2,1)} %param.16) | non-fusion elementwise | flops 2048 | bytes 12288 | tf_op jit(solution)/shard_map/reshape | solution.py:462
  1.9 47.4 %shard_map.131 = (bf16[128,1024]{1,0:T(8,128)(2,1)}, bf16[128,1024]{1,0:T(8,128)(2,1)}) custom-call(bf16[64,4,128]{2,1,0:T(4,128)(2,1)} %pix_hbm.1, s32[1,64]{1,0:T(1,128)} %bitcast.6, bf16[64,2048]{1,0:T(8,128)(2,1)} %emb_ref.1, bf16[8,4,2048]{2,1,0:T(4,128)(2,1)} %gw_hbm.1, f32[1,2048]{1,0:T(1,128)} %bitcast.4, s32[1,128]{1,0:T(1,128)} %bitcast.7, ...), custom_call_target="tpu_custom_call" | custom-call | tf_op jit(solution)/shard_map/pallas_call | solution.py:420
  49.3 1.7 %copy.16 = bf16[128,1024]{1,0:T(8,128)(2,1)} copy(bf16[128,1024]{1,0:T(8,128)(2,1)} %get-tuple-element.4) | data formatting | bytes 524288
  51.0 1.7 %copy.17 = bf16[128,1024]{1,0:T(8,128)(2,1)} copy(bf16[128,1024]{1,0:T(8,128)(2,1)} %get-tuple-element.5) | data formatting | bytes 524288

commit v4 on v3

--- a/solution.py
+++ b/solution.py
@@ -244,7 +244,7 @@
         )
 
     lat_rows = ((NL + 127) // 128) * 128
-    step = 256
+    step = 512
 
     def pieces(x):
         hi = x.astype(BF16)
@@ -267,6 +267,8 @@
             hot = (rows == at_row).astype(F32).T.astype(BF16)[:, :NL]
             split.append(pieces(ck[chip].T) + (hot,))
         hi, mid, low, hot = [jnp.concatenate(x, axis=0) for x in zip(*split)]
+        stacked = jnp.concatenate([low, mid, hi], axis=0)
+        rows_c = C * T
 
         @pl.when(first)
         def _():
@@ -279,9 +281,8 @@
         for j in range(D // step):
             at = slice(j * step, (j + 1) * step)
             base = bm[:, at]
-            part = jnp.dot(low, base, preferred_element_type=F32)
-            part = part + jnp.dot(mid, base, preferred_element_type=F32)
-            part = part + jnp.dot(hi, base, preferred_element_type=F32)
+            three = jnp.dot(stacked, base, preferred_element_type=F32)
+            part = three[0:rows_c] + three[rows_c : 2 * rows_c] + three[2 * rows_c :]
             part = part + jnp.dot(hot, latv[:, at], preferred_element_type=F32)
             lt[:, at] = part
             mean = mean + jnp.sum(part, axis=1, keepdims=True)

time: 52.8 us -> 52.7 us (level)
  the two profiles are of different devices: /device:TPU:22 before, /device:TPU:20 now
where the time goes in v4:
time: 52.7 us; the launch traced here: 52.5 us
  Pallas kernels  47.2 us (90%)
  local copies, waits for them, and re-layouts  3.34 us (6%)
  other arithmetic  1.29 us (2%)
  between operations  0.64 us (1%)
    pallas_call x1, Pallas kernels, on_device(): pl.pallas_call(functools.partial(kernel, S, R, C), out_shape=(out, out),...  47.2 us
    unnamed x2, local copies, waits for them, and re-layouts  3.34 us
    reshape x1, other arithmetic, on_device(): agg_query.astype(F32).reshape(1, D)  1.29 us

profile of v4, /device:TPU:20, one launch (start us, length us, event | category | flops | bytes accessed | tf_op | source)
XLA Modules:
  0.0 52.5 jit_solution(11467648526480652693)
XLA Ops:
  0.6 1.3 %reshape.23 = f32[2048]{0:T(1024)} convert(bf16[2048]{0:T(1024)(128)(2,1)} %param.16) | non-fusion elementwise | flops 2048 | bytes 12288 | tf_op jit(solution)/shard_map/reshape | solution.py:463
  1.9 47.2 %shard_map.131 = (bf16[128,1024]{1,0:T(8,128)(2,1)}, bf16[128,1024]{1,0:T(8,128)(2,1)}) custom-call(bf16[64,4,128]{2,1,0:T(4,128)(2,1)} %pix_hbm.1, s32[1,64]{1,0:T(1,128)} %bitcast.6, bf16[64,2048]{1,0:T(8,128)(2,1)} %emb_ref.1, bf16[8,4,2048]{2,1,0:T(4,128)(2,1)} %gw_hbm.1, f32[1,2048]{1,0:T(1,128)} %bitcast.4, s32[1,128]{1,0:T(1,128)} %bitcast.7, ...), custom_call_target="tpu_custom_call" | custom-call | tf_op jit(solution)/shard_map/pallas_call | solution.py:421
  49.2 1.7 %copy.16 = bf16[128,1024]{1,0:T(8,128)(2,1)} copy(bf16[128,1024]{1,0:T(8,128)(2,1)} %get-tuple-element.4) | data formatting | bytes 524288
  50.8 1.7 %copy.17 = bf16[128,1024]{1,0:T(8,128)(2,1)} copy(bf16[128,1024]{1,0:T(8,128)(2,1)} %get-tuple-element.5) | data formatting | bytes 524288
